TPU v7x, 32 devices: a whole 2x2x4 slice. The times are simulated.
32 devices in a mesh: sec: 4 (over x, core), sub: 8 (over z, y).
Axes of the slice: x: 2, y: 2, z: 4, core: 2. Of those that a mesh axis runs over, the one named last changes fastest.
Arguments:
- schur: bfloat16 [8, 1024, 1024], P('sub', 'sec'), may hold values from -0.1875 to 0.1875
- neumann: bfloat16 [8, 1024, 1024], P('sub', 'sec'), may hold values from -0.1875 to 0.1875
- constraint_weights: bfloat16 [8, 1024, 128], P('sub', 'sec'), may hold values from -0.1875 to 0.1875
- coarse_inverse: bfloat16 [8, 768, 768], P('sub', 'sec'), may hold values from -0.21875 to 0.21875
- solution: bfloat16 [8, 1024, 128], P('sub', 'sec'), may hold values from -6 to 6
- load: bfloat16 [8, 1024, 128], P('sub', 'sec'), may hold values from -6 to 6
- neighbours: int32 [8, 4], P('sub'), may hold values from 0 to 7, as said below
- face_index: int32 [8, 1024], P('sub', 'sec'), may hold values from 0 to 255, as said below
- coarse_dof: int32 [8, 128], P('sub'), may hold values from 0 to 6143, as said below
Outputs:
- precond: bfloat16 [8, 1024, 128], P('sub', 'sec')
- image: bfloat16 [8, 1024, 128], P('sub', 'sec')
Inputs may be any that keep to these rules, and one draw needn't show every extreme that they name: `neighbours`: the subdomain glued to face f of subdomain i is another subdomain whose column c // 1 is the column i // 1 of i or the one before or after it, cyclically over 8 columns. `face_index`: for each subdomain and face, the entries of the face's 256 unknowns are a permutation of 0 to 255. `coarse_dof`: constraint k of subdomain i maps to an unknown of the cluster of column i // 1 or of the column before or after it, cyclically. Each cluster has 64 coarse unknowns that are used, and each used unknown is the unknown of exactly two constraints.
All inputs are finite; a program needn't handle non-finite values.
Results may differ from a plain program's by a relative error of at most 0.0058.
Values may be sent and summed in bfloat16 or wider, within the bound.
No kernel may reach another device: no remote copies, remote signals or barrier semaphores. Data moves between devices by JAX's collectives and lax.ppermute only.
A program may use at most 64 MiB of HBM per device.

v0:
```python
import jax
import jax.numpy as jnp
from jax import lax
from jax.sharding import PartitionSpec as P

F32 = jnp.float32
BF16 = jnp.bfloat16
KINDS = ("A2", "B2", "A3", "B3")


def partner(kind, i, count):
    forward = {
        "A": i % 2 == 0,
        "B": i % 2 == 1,
        "A2": i % 4 < 2,
        "B2": i % 4 >= 2,
        "A3": i % 2 == 0,
        "B3": i % 2 == 1,
    }[kind]
    step = {"2": 2, "3": 3}.get(kind[-1], 1)
    return (i + step if forward else i - step) % count


def swap_columns(array, kind):
    count = lax.axis_size("sub")
    return lax.ppermute(array, "sub", [(i, partner(kind, i, count)) for i in range(count)])


def swap_by_section(array, kinds):
    sections, count = (lax.axis_size("sec"), lax.axis_size("sub"))
    moves = [
        (s * count + i, s * count + partner(kinds[s % len(kinds)], i, count))
        for s in range(sections)
        for i in range(count)
    ]
    return lax.ppermute(array, ("sec", "sub"), moves)


def swap_cores(array):
    return lax.ppermute(array, "sec", [(i, i ^ 1) for i in range(lax.axis_size("sec"))])


def dot(a, b):
    return jnp.dot(a, b, preferred_element_type=F32)


def encode_dof(dof, column, count, coarse_len):
    near = (dof // coarse_len - column + 1) % count
    slot = dof % coarse_len
    parts = -(-coarse_len // 128)
    rows = jnp.stack([near * parts + slot // 128, slot % 128]).astype(BF16)
    return jnp.pad(rows, ((0, 14), (0, 0)))


def decode_dof(rows, offset, coarse_len):
    parts = -(-coarse_len // 128)
    whole = rows[:2].astype(F32).astype(jnp.int32)
    cluster = offset + 1 + whole[0] // parts
    return (cluster, whole[0] % parts * 128 + whole[1])


def local(
    schur,
    neumann,
    constraint_weights,
    coarse_inverse,
    solution,
    load,
    neighbours,
    face_index,
    coarse_dof,
):
    s_rows, n_rows, weights = (schur[0], neumann[0], constraint_weights[0])
    c_rows = coarse_inverse[0]
    face_len, cons = weights.shape
    coarse_part, coarse_len = c_rows.shape
    used = cons // 2
    column, section = (lax.axis_index("sub"), lax.axis_index("sec"))
    count = lax.axis_size("sub")
    core = section % 2
    even = column % 2 == 0
    off1 = jnp.where(even, 1, -1)
    off2 = jnp.where(column % 4 < 2, 2, -2)
    off3 = jnp.where(even, 3, -3)
    own_code = encode_dof(coarse_dof[0], column, count, coarse_len)
    far_code = swap_by_section(own_code, KINDS)
    first = jnp.concatenate([weights, own_code])
    near_b = swap_columns(first, "B")
    near_a = swap_columns(first, "A")
    iterate = lax.all_gather(solution[0], "sec", axis=0, tiled=True)
    residual = load[0].astype(F32) - dot(s_rows, iterate)
    residual_half = residual.astype(BF16)
    res_b = swap_columns(residual_half, "B")
    res_a = swap_columns(residual_half, "A")
    nbr = neighbours[0, section]
    want_a = (nbr - column - off1) % count == 0
    positions = lax.broadcasted_iota(jnp.int32, (face_len, face_len), 1)
    selector = (face_index[0][:, None] == positions).astype(BF16)
    dec = lambda rows, off: decode_dof(rows, off, coarse_len)
    parts3 = [dec(own_code, 0), dec(near_a[face_len:], off1), dec(near_b[face_len:], -off1)]
    clus3 = jnp.concatenate([p[0] for p in parts3])
    slot3 = jnp.concatenate([p[1] for p in parts3])
    key3 = jnp.where(clus3 == 2, slot3, -1)
    less = (key3[None, :] >= 0) & (key3[None, :] < key3[:, None])
    rank3 = jnp.where(key3 >= 0, jnp.sum(less.astype(jnp.int32), axis=1) // 2, -1)
    by_rank = (lax.broadcasted_iota(jnp.int32, (used, 3 * cons), 0) == rank3[None, :]).astype(BF16)
    by_slot = (key3[:, None] == lax.broadcasted_iota(jnp.int32, (3 * cons, coarse_len), 1)).astype(
        BF16
    )
    pick_used = dot(by_rank, by_slot).astype(BF16)
    used_cols = lax.dot_general(
        c_rows, pick_used, (((1,), (1,)), ((), ())), preferred_element_type=F32
    ).astype(BF16)
    pick_rows = lax.dynamic_slice_in_dim(pick_used, section * coarse_part, coarse_part, axis=1)
    used_part = (0.25 * dot(pick_rows, used_cols)).astype(BF16)
    used_part = jnp.pad(used_part, ((0, 0), (0, cons - used)))
    matched = jnp.where(want_a, res_a, res_b)
    assembled = (residual + dot(selector, matched)).astype(BF16)
    values_part = lax.dot_general(
        weights, assembled, (((0,), (0,)), ((), ())), preferred_element_type=F32
    ).astype(BF16)
    packed = jnp.concatenate([assembled, values_part, used_part, far_code])
    around = lax.all_gather(packed, "sec", axis=0)
    assembled_all = around[:, :face_len].reshape(-1, around.shape[2])
    values = jnp.sum(around[:, face_len : face_len + cons].astype(F32), axis=0).astype(BF16)
    at = face_len + cons
    used_block = jnp.sum(around[:, at : at + used].astype(F32), axis=0).astype(BF16)
    far_codes = around[:, at + used :]
    correction = dot(n_rows, assembled_all)
    coarse_load = jnp.concatenate([values, used_block])
    out = jnp.concatenate([correction.astype(BF16), coarse_load])
    far2_mine = swap_by_section(coarse_load, KINDS[:2])
    far3_mine = swap_by_section(values, KINDS[2:])
    cor_b = swap_columns(out, "B")
    cor_a = swap_columns(out, "A")
    far_mine = jnp.concatenate([far2_mine, far3_mine])
    far_other = swap_cores(far_mine)
    sign = jnp.where(core == 0, 1, -1)
    c0 = lambda x, y: jnp.where(core == 0, x, y)
    window = parts3 + [
        dec(c0(far_codes[0], far_codes[1]), sign * off2),
        dec(c0(far_codes[1], far_codes[0]), -sign * off2),
        dec(c0(far_codes[2], far_codes[3]), sign * off3),
        dec(c0(far_codes[3], far_codes[2]), -sign * off3),
    ]
    clus = jnp.concatenate([p[0] for p in window])
    slot = jnp.concatenate([p[1] for p in window])
    inside = (clus >= 0) & (clus < 5)
    same_less = (clus[None, :] == clus[:, None]) & (slot[None, :] < slot[:, None])
    rank = jnp.sum(same_less.astype(jnp.int32), axis=1) // 2
    order = [0, off1, -off1, sign * off2, -sign * off2]
    place = sum((jnp.where(clus == 2 + order[m], m, 0) for m in range(1, 5)))
    code = jnp.where(inside, place * used + rank, -1)
    unknowns = 5 * used
    spread = (lax.broadcasted_iota(jnp.int32, (unknowns, 7 * cons), 0) == code[None, :]).astype(
        BF16
    )
    nbr_code = jnp.where(want_a, code[cons : 2 * cons], code[2 * cons : 3 * cons])
    pair_code = jnp.concatenate([code[:cons], nbr_code])
    gather = (
        pair_code[:, None] == lax.broadcasted_iota(jnp.int32, (2 * cons, unknowns), 1)
    ).astype(BF16)
    weights_nbr = jnp.where(want_a, near_a[:face_len], near_b[:face_len])
    weights_pair = jnp.concatenate([weights, dot(selector, weights_nbr).astype(BF16)], axis=1)
    far = coarse_load.shape[0]
    values_near = jnp.concatenate(
        [
            values,
            cor_a[face_len : face_len + cons],
            cor_b[face_len : face_len + cons],
            far_mine[:cons],
            far_other[:cons],
            far_mine[far:],
            far_other[far:],
        ]
    )
    blocks = jnp.stack(
        [
            used_block,
            cor_a[face_len + cons :],
            cor_b[face_len + cons :],
            far_mine[cons:far],
            far_other[cons:far],
        ]
    )[:, :, :used]
    rhs = dot(spread, values_near).astype(BF16).reshape(5, used, -1)
    coarse = jnp.einsum("quv,qvc->quc", blocks, rhs, preferred_element_type=F32).astype(BF16)
    picked = dot(gather, coarse.reshape(unknowns, -1)).astype(BF16)
    facing = dot(selector, jnp.where(want_a, cor_a[:face_len], cor_b[:face_len]))
    precond = (0.5 * (correction + facing + dot(weights_pair, picked))).astype(BF16)
    precond_all = lax.all_gather(precond, "sec", axis=0, tiled=True)
    image = dot(s_rows, precond_all).astype(BF16)
    return (precond[None], image[None])


def solution(mesh):
    placed = (
        P("sub", "sec", None),
        P("sub", "sec", None),
        P("sub", "sec", None),
        P("sub", "sec", None),
        P("sub", "sec", None),
        P("sub", "sec", None),
        P("sub", None),
        P("sub", "sec"),
        P("sub", None),
    )
    return jax.shard_map(
        local,
        mesh=mesh,
        in_specs=placed,
        out_specs=(P("sub", "sec", None), P("sub", "sec", None)),
        check_vma=False,
    )
```

profile of v0, /device:TPU:0, one launch (start us, length us, event | category | flops | bytes accessed | tf_op | source)
XLA Modules:
  0.0 52.0 jit_solution(424004631807403690)
XLA Ops:
  0.6 0.0 copy-start
  0.6 0.0 copy-start.5
  0.7 0.7 %fusion.84 = (bf16[1,128]{1,0:T(2,128)(2,1)S(1)}, s32[1,128]{1,0:T(1,128)S(1)}) fusion(s32[1,128]{1,0:T(1,128)} %param.17, s32[]{:T(128)S(6)} %axis_index.25), kind=kLoop, calls=%fused_computation.216 | loop fusion | flops 5504 | bytes 1284 | tf_op jit(solution)/shard_map/convert.3
  1.4 3.1 %collective-permute-start.4 = (bf16[16,128]{1,0:T(8,128)(2,1)S(1)}, bf16[16,128]{1,0:T(8,128)(2,1)S(1)}, u32[]{:S(2)}, u32[]{:S(2)}) collective-permute-start(bf16[16,128]{1,0:T(8,128)(2,1)S(1)} %pad.8), channel_id=1, source_target_pairs={{0,2},{1,3},{2,0},{3,1},{4,6},{5,7},{6,4},{7,5},{8,14},{9,15},{10,... | collective-permute-start | bytes 12296 | tf_op jit(solution)/shard_map/ppermute | solution.py:36
  4.6 0.8 %pad_maximum_fusion.2 = bf16[272,128]{1,0:T(8,128)(2,1)S(1)} fusion(bf16[16,128]{1,0:T(8,128)(2,1)S(1)} %pad.8, bf16[256,128]{1,0:T(8,128)(2,1)} %bitcast.261), kind=kLoop, calls=%fused_computation.54 | loop fusion | flops 139264 | bytes 139264 | tf_op jit(solution)/shard_map/concatenate | solution.py:87
  5.4 3.4 %collective-permute-start.3 = (bf16[272,128]{1,0:T(8,128)(2,1)S(1)}, bf16[272,128]{1,0:T(8,128)(2,1)S(1)}, u32[]{:S(2)}, u32[]{:S(2)}) collective-permute-start(bf16[272,128]{1,0:T(8,128)(2,1)S(1)} %pad_maximum_fusion.2), channel_id=1, source_target_pairs={{0,7},{1,2},{2,1},{3,4},{4,3},{5,6},{6,5},{7,0},{8,15},{9,10},{10,... | collective-permute-start | bytes 208904 | tf_op jit(solution)/shard_map/ppermute | solution.py:26
  8.8 0.0 collective-permute-start.2
  8.8 6.5 %all-gather = bf16[1,1024,128]{2,1,0:T(8,128)(2,1)S(1)} all-gather(bf16[1,256,128]{2,1,0:T(8,128)(2,1)} %param.13), channel_id=2, replica_groups=mesh['sec'=4,'sub'=8] {'sec'}, dimensions={1}, use_global_device_ids=true | all-gather | bytes 327680 | tf_op jit(solution)/shard_map/all_gather | solution.py:90
  15.3 0.0 copy-done
  15.3 0.0 copy-done.5
  15.4 0.0 copy-start.3
  15.4 0.3 fusion.95
  15.7 2.6 %collective-permute-start.1 = (bf16[256,128]{1,0:T(8,128)(2,1)S(1)}, bf16[256,128]{1,0:T(8,128)(2,1)S(1)}, u32[]{:S(2)}, u32[]{:S(2)}) collective-permute-start(bf16[256,128]{1,0:T(8,128)(2,1)S(1)} %get-tuple-element.63), channel_id=1, source_target_pairs={{0,7},{1,2},{2,1},{3,4},{4,3},{5,6},{6,5},{7,0},{8,15},{9,10},{10,... | collective-permute-start | bytes 196616 | tf_op jit(solution)/shard_map/ppermute | solution.py:26
  18.2 0.5 %collective-permute-start = (bf16[256,128]{1,0:T(8,128)(2,1)S(1)}, bf16[256,128]{1,0:T(8,128)(2,1)S(1)}, u32[]{:S(2)}, u32[]{:S(2)}) collective-permute-start(bf16[256,128]{1,0:T(8,128)(2,1)S(1)} %get-tuple-element.63), channel_id=1, source_target_pairs={{0,1},{1,0},{2,3},{3,2},{4,5},{5,4},{6,7},{7,6},{8,9},{9,8},{10,11... | collective-permute-start | bytes 196616 | tf_op jit(solution)/shard_map/ppermute | solution.py:26
  18.9 0.6 %constant_dynamic-slice_fusion = s32[1,1]{1,0:T(1,128)} fusion(s32[1,4]{1,0:T(1,128)S(1)} %copy-done.7, s32[]{:T(128)S(6)} %select_n.297), kind=kLoop, calls=%fused_computation.209 | loop fusion | bytes 12 | tf_op jit(solution)/shard_map/dynamic_slice | solution.py:95
  20.1 0.0 copy-start.2
  20.2 2.7 %collective-permute-done.1 = bf16[256,128]{1,0:T(8,128)(2,1)S(1)} collective-permute-done((bf16[256,128]{1,0:T(8,128)(2,1)S(1)}, bf16[256,128]{1,0:T(8,128)(2,1)S(1)}, u32[]{:S(2)}, u32[]{:S(2)}) %collective-permute-start.1) | collective-permute-done | bytes 65568 | tf_op jit(solution)/shard_map/ppermute | solution.py:26
  22.9 0.8 %collective-permute-done = bf16[256,128]{1,0:T(8,128)(2,1)S(1)} collective-permute-done((bf16[256,128]{1,0:T(8,128)(2,1)S(1)}, bf16[256,128]{1,0:T(8,128)(2,1)S(1)}, u32[]{:S(2)}, u32[]{:S(2)}) %collective-permute-start) | collective-permute-done | bytes 65568 | tf_op jit(solution)/shard_map/ppermute | solution.py:26
  23.7 0.2 fusion.7
  24.0 0.2 fusion.10
  24.2 0.0 collective-permute-done.3
  24.2 0.0 collective-permute-done.2
  24.4 0.2 convert_reduce_fusion.1
  24.7 0.4 fusion.2
  25.1 0.4 fusion.11
  25.5 0.0 collective-permute-done.4
  25.5 6.4 %all-gather.1 = bf16[1856,128]{1,0:T(8,128)(2,1)S(1)} all-gather(bf16[464,128]{1,0:T(8,128)(2,1)S(1)} %fusion.31), channel_id=3, replica_groups=mesh['sec'=4,'sub'=8] {'sec'}, dimensions={0}, use_global_device_ids=true | all-gather | bytes 593920 | tf_op jit(solution)/shard_map/all_gather | solution.py:123
  32.0 1.0 %collective-permute-start.8 = (bf16[128,128]{1,0:T(8,128)(2,1)S(1)}, bf16[128,128]{1,0:T(8,128)(2,1)S(1)}, u32[]{:S(2)}, u32[]{:S(2)}) collective-permute-start(bf16[128,128]{1,0:T(8,128)(2,1)S(1)} %slice_reduce_fusion), channel_id=1, source_target_pairs={{0,3},{1,6},{2,5},{3,0},{4,7},{5,2},{6,1},{7,4},{8,13},{9,12},{10,... | collective-permute-start | bytes 98312 | tf_op jit(solution)/shard_map/ppermute | solution.py:36
  33.0 0.3 fusion.96
  33.3 2.7 %collective-permute-start.6 = (bf16[448,128]{1,0:T(8,128)(2,1)S(1)}, bf16[448,128]{1,0:T(8,128)(2,1)S(1)}, u32[]{:S(2)}, u32[]{:S(2)}) collective-permute-start(bf16[448,128]{1,0:T(8,128)(2,1)S(1)} %pad_maximum_fusion), channel_id=1, source_target_pairs={{0,7},{1,2},{2,1},{3,4},{4,3},{5,6},{6,5},{7,0},{8,15},{9,10},{10,... | collective-permute-start | bytes 344072 | tf_op jit(solution)/shard_map/ppermute | solution.py:26
  36.0 0.0 collective-permute-start.5
  36.1 0.7 %convert_reduce_fusion = s32[896]{0:T(1024)S(1)} fusion(s32[896]{0:T(1024)S(1)} %get-tuple-element.46, s32[896]{0:T(1024)S(1)} %get-tuple-element.45), kind=kLoop, calls=%fused_computation | loop fusion | flops 4013184 | bytes 10752 | tf_op jit(solution)/shard_map/reduce_sum | solution.py:150
  36.9 1.8 %collective-permute-start.7 = (bf16[192,128]{1,0:T(8,128)(2,1)S(1)}, bf16[192,128]{1,0:T(8,128)(2,1)S(1)}, u32[]{:S(2)}, u32[]{:S(2)}) collective-permute-start(bf16[192,128]{1,0:T(8,128)(2,1)S(1)} %pad_maximum_fusion.3), channel_id=1, source_target_pairs={{0,2},{1,3},{2,0},{3,1},{4,6},{5,7},{6,4},{7,5},{8,14},{9,15},{10,... | collective-permute-start | bytes 147464 | tf_op jit(solution)/shard_map/ppermute | solution.py:36
  38.6 0.2 convolution_convert_fusion.3
  38.9 0.0 collective-permute-done.8
  38.9 2.1 %collective-permute-done.7 = bf16[192,128]{1,0:T(8,128)(2,1)S(1)} collective-permute-done((bf16[192,128]{1,0:T(8,128)(2,1)S(1)}, bf16[192,128]{1,0:T(8,128)(2,1)S(1)}, u32[]{:S(2)}, u32[]{:S(2)}) %collective-permute-start.7) | collective-permute-done | bytes 49184 | tf_op jit(solution)/shard_map/ppermute | solution.py:36
  41.0 1.6 %collective-permute-start.9 = (bf16[320,128]{1,0:T(8,128)(2,1)S(1)}, bf16[320,128]{1,0:T(8,128)(2,1)S(1)}, u32[]{:S(2)}, u32[]{:S(2)}) collective-permute-start(bf16[320,128]{1,0:T(8,128)(2,1)S(1)} %pad_maximum_fusion.1), channel_id=1, source_target_pairs={{0,8},{8,0},{16,24},{24,16},{1,9},{9,1},{17,25},{25,17},{2,10},{10... | collective-permute-start | bytes 245768 | tf_op jit(solution)/shard_map/ppermute | solution.py:40
  42.6 1.2 %collective-permute-done.5 = bf16[448,128]{1,0:T(8,128)(2,1)S(1)} collective-permute-done((bf16[448,128]{1,0:T(8,128)(2,1)S(1)}, bf16[448,128]{1,0:T(8,128)(2,1)S(1)}, u32[]{:S(2)}, u32[]{:S(2)}) %collective-permute-start.5) | collective-permute-done | bytes 114720 | tf_op jit(solution)/shard_map/ppermute | solution.py:26
  43.8 0.0 collective-permute-done.6
  43.9 0.0 collective-permute-done.9
  43.9 0.3 fusion.5
  44.3 0.1 convolution_convert_fusion
  44.4 0.5 fusion.9
  44.9 0.2 fusion.6
  45.1 0.0 copy-start.4
  45.1 5.8 %all_gather.15 = bf16[1024,128]{1,0:T(8,128)(2,1)S(1)} all-gather(bf16[256,128]{1,0:T(8,128)(2,1)S(1)} %fusion.6), channel_id=1, replica_groups=mesh['sec'=4,'sub'=8] {'sec'}, dimensions={0}, use_global_device_ids=true | all-gather | bytes 327680 | tf_op jit(solution)/shard_map/all_gather | solution.py:191
  50.9 0.3 fusion.8
  51.3 0.7 %copy.14 = bf16[1,256,128]{2,1,0:T(8,128)(2,1)} copy(bf16[1,256,128]{1,2,0:T(8,128)(2,1)S(1)} %fusion.8) | data formatting | bytes 131072
  (57 shorter events, 0.6 us)
Async XLA Ops:
  0.6 14.7 %copy-start = (bf16[1,256,1024]{2,1,0:T(8,128)(2,1)S(1)}, bf16[1,256,1024]{2,1,0:T(8,128)(2,1)}, u32[]{:S(2)}) copy-start(bf16[1,256,1024]{2,1,0:T(8,128)(2,1)} %param.9) | copy-start | bytes 1572868
  0.6 14.7 %copy-start.5 = (bf16[1,256,128]{2,1,0:T(8,128)(2,1)S(1)}, bf16[1,256,128]{2,1,0:T(8,128)(2,1)}, u32[]{:S(2)}) copy-start(bf16[1,256,128]{2,1,0:T(8,128)(2,1)} %param.14) | copy-start | bytes 196612
  1.4 24.0 %collective-permute-start.4 = (bf16[16,128]{1,0:T(8,128)(2,1)S(1)}, bf16[16,128]{1,0:T(8,128)(2,1)S(1)}, u32[]{:S(2)}, u32[]{:S(2)}) collective-permute-start(bf16[16,128]{1,0:T(8,128)(2,1)S(1)} %pad.8), channel_id=1, source_target_pairs={{0,2},{1,3},{2,0},{3,1},{4,6},{5,7},{6,4},{7,5},{8,14},{9,15},{10,... | collective-permute-start | bytes 12296 | tf_op jit(solution)/shard_map/ppermute | solution.py:36
  5.4 18.8 %collective-permute-start.3 = (bf16[272,128]{1,0:T(8,128)(2,1)S(1)}, bf16[272,128]{1,0:T(8,128)(2,1)S(1)}, u32[]{:S(2)}, u32[]{:S(2)}) collective-permute-start(bf16[272,128]{1,0:T(8,128)(2,1)S(1)} %pad_maximum_fusion.2), channel_id=1, source_target_pairs={{0,7},{1,2},{2,1},{3,4},{4,3},{5,6},{6,5},{7,0},{8,15},{9,10},{10,... | collective-permute-start | bytes 208904 | tf_op jit(solution)/shard_map/ppermute | solution.py:26
  8.8 15.4 %collective-permute-start.2 = (bf16[272,128]{1,0:T(8,128)(2,1)S(1)}, bf16[272,128]{1,0:T(8,128)(2,1)S(1)}, u32[]{:S(2)}, u32[]{:S(2)}) collective-permute-start(bf16[272,128]{1,0:T(8,128)(2,1)S(1)} %pad_maximum_fusion.2), channel_id=1, source_target_pairs={{0,1},{1,0},{2,3},{3,2},{4,5},{5,4},{6,7},{7,6},{8,9},{9,8},{10,11... | collective-permute-start | bytes 208904 | tf_op jit(solution)/shard_map/ppermute | solution.py:26
  15.3 3.5 %copy-start.7 = (s32[1,4]{1,0:T(1,128)S(1)}, s32[1,4]{1,0:T(1,128)}, u32[]{:S(2)}) copy-start(s32[1,4]{1,0:T(1,128)} %param.15) | copy-start | bytes 52
  15.4 8.4 %copy-start.6 = (s32[1,256]{1,0:T(1,128)S(1)}, s32[1,256]{1,0:T(1,128)}, u32[]{:S(2)}) copy-start(s32[1,256]{1,0:T(1,128)} %param.16) | copy-start | bytes 3076
  15.4 8.6 %copy-start.3 = (bf16[1,256,128]{2,1,0:T(8,128)(2,1)S(1)}, bf16[1,256,128]{2,1,0:T(8,128)(2,1)}, u32[]{:S(2)}) copy-start(bf16[1,256,128]{2,1,0:T(8,128)(2,1)} %param.11) | copy-start | bytes 196612
  15.7 7.2 %collective-permute-start.1 = (bf16[256,128]{1,0:T(8,128)(2,1)S(1)}, bf16[256,128]{1,0:T(8,128)(2,1)S(1)}, u32[]{:S(2)}, u32[]{:S(2)}) collective-permute-start(bf16[256,128]{1,0:T(8,128)(2,1)S(1)} %get-tuple-element.63), channel_id=1, source_target_pairs={{0,7},{1,2},{2,1},{3,4},{4,3},{5,6},{6,5},{7,0},{8,15},{9,10},{10,... | collective-permute-start | bytes 196616 | tf_op jit(solution)/shard_map/ppermute | solution.py:26
  18.2 5.5 %collective-permute-start = (bf16[256,128]{1,0:T(8,128)(2,1)S(1)}, bf16[256,128]{1,0:T(8,128)(2,1)S(1)}, u32[]{:S(2)}, u32[]{:S(2)}) collective-permute-start(bf16[256,128]{1,0:T(8,128)(2,1)S(1)} %get-tuple-element.63), channel_id=1, source_target_pairs={{0,1},{1,0},{2,3},{3,2},{4,5},{5,4},{6,7},{7,6},{8,9},{9,8},{10,11... | collective-permute-start | bytes 196616 | tf_op jit(solution)/shard_map/ppermute | solution.py:26
  20.1 4.9 %copy-start.2 = (bf16[1,192,768]{2,1,0:T(8,128)(2,1)S(1)}, bf16[1,192,768]{2,1,0:T(8,128)(2,1)}, u32[]{:S(2)}) copy-start(bf16[1,192,768]{2,1,0:T(8,128)(2,1)} %param.12) | copy-start | bytes 884740
  31.9 1.1 %copy-start.1 = (bf16[1,256,1024]{2,1,0:T(8,128)(2,1)S(1)}, bf16[1,256,1024]{2,1,0:T(8,128)(2,1)}, u32[]{:S(2)}) copy-start(bf16[1,256,1024]{2,1,0:T(8,128)(2,1)} %param.10) | copy-start | bytes 1572868
  32.0 7.0 %collective-permute-start.8 = (bf16[128,128]{1,0:T(8,128)(2,1)S(1)}, bf16[128,128]{1,0:T(8,128)(2,1)S(1)}, u32[]{:S(2)}, u32[]{:S(2)}) collective-permute-start(bf16[128,128]{1,0:T(8,128)(2,1)S(1)} %slice_reduce_fusion), channel_id=1, source_target_pairs={{0,3},{1,6},{2,5},{3,0},{4,7},{5,2},{6,1},{7,4},{8,13},{9,12},{10,... | collective-permute-start | bytes 98312 | tf_op jit(solution)/shard_map/ppermute | solution.py:36
  33.3 10.5 %collective-permute-start.6 = (bf16[448,128]{1,0:T(8,128)(2,1)S(1)}, bf16[448,128]{1,0:T(8,128)(2,1)S(1)}, u32[]{:S(2)}, u32[]{:S(2)}) collective-permute-start(bf16[448,128]{1,0:T(8,128)(2,1)S(1)} %pad_maximum_fusion), channel_id=1, source_target_pairs={{0,7},{1,2},{2,1},{3,4},{4,3},{5,6},{6,5},{7,0},{8,15},{9,10},{10,... | collective-permute-start | bytes 344072 | tf_op jit(solution)/shard_map/ppermute | solution.py:26
  36.0 7.8 %collective-permute-start.5 = (bf16[448,128]{1,0:T(8,128)(2,1)S(1)}, bf16[448,128]{1,0:T(8,128)(2,1)S(1)}, u32[]{:S(2)}, u32[]{:S(2)}) collective-permute-start(bf16[448,128]{1,0:T(8,128)(2,1)S(1)} %pad_maximum_fusion), channel_id=1, source_target_pairs={{0,1},{1,0},{2,3},{3,2},{4,5},{5,4},{6,7},{7,6},{8,9},{9,8},{10,11... | collective-permute-start | bytes 344072 | tf_op jit(solution)/shard_map/ppermute | solution.py:26
  36.9 4.2 %collective-permute-start.7 = (bf16[192,128]{1,0:T(8,128)(2,1)S(1)}, bf16[192,128]{1,0:T(8,128)(2,1)S(1)}, u32[]{:S(2)}, u32[]{:S(2)}) collective-permute-start(bf16[192,128]{1,0:T(8,128)(2,1)S(1)} %pad_maximum_fusion.3), channel_id=1, source_target_pairs={{0,2},{1,3},{2,0},{3,1},{4,6},{5,7},{6,4},{7,5},{8,14},{9,15},{10,... | collective-permute-start | bytes 147464 | tf_op jit(solution)/shard_map/ppermute | solution.py:36
  41.0 2.8 %collective-permute-start.9 = (bf16[320,128]{1,0:T(8,128)(2,1)S(1)}, bf16[320,128]{1,0:T(8,128)(2,1)S(1)}, u32[]{:S(2)}, u32[]{:S(2)}) collective-permute-start(bf16[320,128]{1,0:T(8,128)(2,1)S(1)} %pad_maximum_fusion.1), channel_id=1, source_target_pairs={{0,8},{8,0},{16,24},{24,16},{1,9},{9,1},{17,25},{25,17},{2,10},{10... | collective-permute-start | bytes 245768 | tf_op jit(solution)/shard_map/ppermute | solution.py:40
  45.1 6.1 %copy-start.4 = (bf16[256,128]{1,0:T(8,128)(2,1)}, bf16[256,128]{1,0:T(8,128)(2,1)S(1)}, u32[]{:S(2)}) copy-start(bf16[256,128]{1,0:T(8,128)(2,1)S(1)} %fusion.6) | copy-start | bytes 196612
where the time goes:
time: 52.2 us; the launch traced here: 52 us
  blocking collectives  18.6 us (36%)
  starting transfers between devices  16.7 us (32%)
  waiting for transfers between devices  6.86 us (13%)
  matrix products  3.55 us (7%)
  other arithmetic  2.93 us (6%)
  between operations  1.77 us (3%)
  local copies, waits for them, and re-layouts  1.5 us (3%)
    ppermute x6, starting transfers between devices, swap_columns(): lax.ppermute(array, 'sub', [(i, partner(kind, i, count)) for i in range(c...  9.27 us
    all_gather x1, blocking collectives, local(): iterate = lax.all_gather(solution[0], 'sec', axis=0, tiled=True)  6.5 us
    all_gather x1, blocking collectives, local(): around = lax.all_gather(packed, 'sec', axis=0)  6.37 us
    ppermute x3, starting transfers between devices, swap_by_section(): return lax.ppermute(array, ('sec', 'sub'), moves)  5.91 us
    all_gather x1, blocking collectives, local(): precond_all = lax.all_gather(precond, 'sec', axis=0, tiled=True)  5.78 us
    ppermute x6, waiting for transfers between devices, swap_columns(): lax.ppermute(array, 'sub', [(i, partner(kind, i, count)) for i in range(c...  4.73 us
    dot_general x10, matrix products, dot(): return jnp.dot(a, b, preferred_element_type=F32)  3.18 us
    ppermute x3, waiting for transfers between devices, swap_by_section(): return lax.ppermute(array, ('sec', 'sub'), moves)  2.13 us
  transfers between devices with their start and end apart: 10, of which 4 were waited for; matrix products, arithmetic and copies ran while one was open for 9% of the time, Pallas kernels for 0%

commit v1 on v0

--- a/solution.py
+++ b/solution.py
@@ -188,7 +188,12 @@
     picked = dot(gather, coarse.reshape(unknowns, -1)).astype(BF16)
     facing = dot(selector, jnp.where(want_a, cor_a[:face_len], cor_b[:face_len]))
     precond = (0.5 * (correction + facing + dot(weights_pair, picked))).astype(BF16)
-    precond_all = lax.all_gather(precond, "sec", axis=0, tiled=True)
+    ring = [precond]
+    for hop in range(3):
+        ring.append(lax.ppermute(ring[-1], "sec", [(dev, (dev + 1) % 4) for dev in range(4)]))
+    precond_all = jnp.roll(
+        jnp.concatenate(ring[::-1], axis=0), (lax.axis_index("sec") + 1) * ring[0].shape[0], axis=0
+    )
     image = dot(s_rows, precond_all).astype(BF16)
     return (precond[None], image[None])
 

time: 52.2 us -> 57.7 us (1.11)
  waiting for transfers between devices: 6.86 us -> 17.9 us
  blocking collectives: 18.6 us -> 12.9 us
    ppermute x0 -> x3, waiting for transfers between devices: none -> 11.1 us  [local(): lax.ppermute(ring[-1], 'sec', [(dev, (dev + 1) % 4) for dev in range(4)])]
    all_gather x1 -> x0, blocking collectives: 5.78 us -> none  [local(): precond_all = lax.all_gather(precond, 'sec', axis=0, tiled=True)]
  transfers between devices with their start and end apart: 10 -> 13, of which waited for: 4 -> 7; matrix products, arithmetic and copies ran while one was open for 9% -> 8% of each run, Pallas kernels for 0% -> 0%
where the time goes in v1:
time: 57.7 us; the launch traced here: 57.5 us
  waiting for transfers between devices  17.9 us (31%)
  starting transfers between devices  16.8 us (29%)
  blocking collectives  12.9 us (22%)
  matrix products  3.55 us (6%)
  other arithmetic  2.93 us (5%)
  between operations  1.81 us (3%)
  local copies, waits for them, and re-layouts  1.6 us (3%)
    ppermute x3, waiting for transfers between devices, local(): lax.ppermute(ring[-1], 'sec', [(dev, (dev + 1) % 4) for dev in range(4)])  11.1 us
    ppermute x6, starting transfers between devices, swap_columns(): lax.ppermute(array, 'sub', [(i, partner(kind, i, count)) for i in range(c...  9.27 us
    all_gather x1, blocking collectives, local(): iterate = lax.all_gather(solution[0], 'sec', axis=0, tiled=True)  6.5 us
    all_gather x1, blocking collectives, local(): around = lax.all_gather(packed, 'sec', axis=0)  6.37 us
    ppermute x3, starting transfers between devices, swap_by_section(): return lax.ppermute(array, ('sec', 'sub'), moves)  5.91 us
    ppermute x6, waiting for transfers between devices, swap_columns(): lax.ppermute(array, 'sub', [(i, partner(kind, i, count)) for i in range(c...  4.73 us
    dot_general x10, matrix products, dot(): return jnp.dot(a, b, preferred_element_type=F32)  3.19 us
    ppermute x3, waiting for transfers between devices, swap_by_section(): return lax.ppermute(array, ('sec', 'sub'), moves)  2.13 us
  transfers between devices with their start and end apart: 13, of which 7 were waited for; matrix products, arithmetic and copies ran while one was open for 8% of the time, Pallas kernels for 0%

profile of v1, /device:TPU:0, one launch (start us, length us, event | category | flops | bytes accessed | tf_op | source)
XLA Modules:
  0.0 57.5 jit_solution(16660198952854463232)
XLA Ops:
  0.6 0.0 copy-start
  0.7 0.7 %fusion.86 = (bf16[1,128]{1,0:T(2,128)(2,1)S(1)}, s32[1,128]{1,0:T(1,128)S(1)}) fusion(s32[1,128]{1,0:T(1,128)} %param.17, s32[]{:T(128)S(6)} %axis_index.29), kind=kLoop, calls=%fused_computation.226 | loop fusion | flops 5504 | bytes 1284 | tf_op jit(solution)/shard_map/convert.3
  1.4 3.1 %collective-permute-start.4 = (bf16[16,128]{1,0:T(8,128)(2,1)S(1)}, bf16[16,128]{1,0:T(8,128)(2,1)S(1)}, u32[]{:S(2)}, u32[]{:S(2)}) collective-permute-start(bf16[16,128]{1,0:T(8,128)(2,1)S(1)} %pad.8), channel_id=1, source_target_pairs={{0,2},{1,3},{2,0},{3,1},{4,6},{5,7},{6,4},{7,5},{8,14},{9,15},{10,... | collective-permute-start | bytes 12296 | tf_op jit(solution)/shard_map/ppermute | solution.py:36
  4.6 0.8 %pad_maximum_fusion.2 = bf16[272,128]{1,0:T(8,128)(2,1)S(1)} fusion(bf16[16,128]{1,0:T(8,128)(2,1)S(1)} %pad.8, bf16[256,128]{1,0:T(8,128)(2,1)} %bitcast.261), kind=kLoop, calls=%fused_computation.55 | loop fusion | flops 139264 | bytes 139264 | tf_op jit(solution)/shard_map/concatenate | solution.py:87
  5.4 3.4 %collective-permute-start.3 = (bf16[272,128]{1,0:T(8,128)(2,1)S(1)}, bf16[272,128]{1,0:T(8,128)(2,1)S(1)}, u32[]{:S(2)}, u32[]{:S(2)}) collective-permute-start(bf16[272,128]{1,0:T(8,128)(2,1)S(1)} %pad_maximum_fusion.2), channel_id=1, source_target_pairs={{0,7},{1,2},{2,1},{3,4},{4,3},{5,6},{6,5},{7,0},{8,15},{9,10},{10,... | collective-permute-start | bytes 208904 | tf_op jit(solution)/shard_map/ppermute | solution.py:26
  8.8 0.0 collective-permute-start.2
  8.8 6.5 %all-gather = bf16[1,1024,128]{2,1,0:T(8,128)(2,1)S(1)} all-gather(bf16[1,256,128]{2,1,0:T(8,128)(2,1)} %param.13), channel_id=2, replica_groups=mesh['sec'=4,'sub'=8] {'sec'}, dimensions={1}, use_global_device_ids=true | all-gather | bytes 327680 | tf_op jit(solution)/shard_map/all_gather | solution.py:90
  15.4 0.0 copy-start.4
  15.4 0.3 fusion.97
  15.7 2.6 %collective-permute-start.1 = (bf16[256,128]{1,0:T(8,128)(2,1)S(1)}, bf16[256,128]{1,0:T(8,128)(2,1)S(1)}, u32[]{:S(2)}, u32[]{:S(2)}) collective-permute-start(bf16[256,128]{1,0:T(8,128)(2,1)S(1)} %get-tuple-element.63), channel_id=1, source_target_pairs={{0,7},{1,2},{2,1},{3,4},{4,3},{5,6},{6,5},{7,0},{8,15},{9,10},{10,... | collective-permute-start | bytes 196616 | tf_op jit(solution)/shard_map/ppermute | solution.py:26
  18.2 0.5 collective-permute-start
  18.9 0.6 %constant_dynamic-slice_fusion = s32[1,1]{1,0:T(1,128)} fusion(s32[1,4]{1,0:T(1,128)S(1)} %copy-done.7, s32[]{:T(128)S(6)} %select_n.309), kind=kLoop, calls=%fused_computation.191 | loop fusion | bytes 12 | tf_op jit(solution)/shard_map/dynamic_slice | solution.py:95
  20.1 0.0 copy-start.3
  20.2 2.7 %collective-permute-done.1 = bf16[256,128]{1,0:T(8,128)(2,1)S(1)} collective-permute-done((bf16[256,128]{1,0:T(8,128)(2,1)S(1)}, bf16[256,128]{1,0:T(8,128)(2,1)S(1)}, u32[]{:S(2)}, u32[]{:S(2)}) %collective-permute-start.1) | collective-permute-done | bytes 65568 | tf_op jit(solution)/shard_map/ppermute | solution.py:26
  22.9 0.8 %collective-permute-done = bf16[256,128]{1,0:T(8,128)(2,1)S(1)} collective-permute-done((bf16[256,128]{1,0:T(8,128)(2,1)S(1)}, bf16[256,128]{1,0:T(8,128)(2,1)S(1)}, u32[]{:S(2)}, u32[]{:S(2)}) %collective-permute-start) | collective-permute-done | bytes 65568 | tf_op jit(solution)/shard_map/ppermute | solution.py:26
  23.7 0.2 fusion.7
  24.0 0.2 fusion.10
  24.2 0.0 collective-permute-done.3
  24.2 0.0 collective-permute-done.2
  24.4 0.2 convert_reduce_fusion.1
  24.7 0.4 fusion.2
  25.1 0.4 fusion.11
  25.5 0.0 collective-permute-done.4
  25.5 6.4 %all-gather.1 = bf16[1856,128]{1,0:T(8,128)(2,1)S(1)} all-gather(bf16[464,128]{1,0:T(8,128)(2,1)S(1)} %fusion.32), channel_id=3, replica_groups=mesh['sec'=4,'sub'=8] {'sec'}, dimensions={0}, use_global_device_ids=true | all-gather | bytes 593920 | tf_op jit(solution)/shard_map/all_gather | solution.py:123
  32.0 1.0 %collective-permute-start.8 = (bf16[128,128]{1,0:T(8,128)(2,1)S(1)}, bf16[128,128]{1,0:T(8,128)(2,1)S(1)}, u32[]{:S(2)}, u32[]{:S(2)}) collective-permute-start(bf16[128,128]{1,0:T(8,128)(2,1)S(1)} %slice_reduce_fusion), channel_id=1, source_target_pairs={{0,3},{1,6},{2,5},{3,0},{4,7},{5,2},{6,1},{7,4},{8,13},{9,12},{10,... | collective-permute-start | bytes 98312 | tf_op jit(solution)/shard_map/ppermute | solution.py:36
  33.0 0.3 fusion.98
  33.3 2.7 %collective-permute-start.6 = (bf16[448,128]{1,0:T(8,128)(2,1)S(1)}, bf16[448,128]{1,0:T(8,128)(2,1)S(1)}, u32[]{:S(2)}, u32[]{:S(2)}) collective-permute-start(bf16[448,128]{1,0:T(8,128)(2,1)S(1)} %pad_maximum_fusion), channel_id=1, source_target_pairs={{0,7},{1,2},{2,1},{3,4},{4,3},{5,6},{6,5},{7,0},{8,15},{9,10},{10,... | collective-permute-start | bytes 344072 | tf_op jit(solution)/shard_map/ppermute | solution.py:26
  36.0 0.0 collective-permute-start.5
  36.1 0.7 %convert_reduce_fusion = s32[896]{0:T(1024)S(1)} fusion(s32[896]{0:T(1024)S(1)} %get-tuple-element.46, s32[896]{0:T(1024)S(1)} %get-tuple-element.45), kind=kLoop, calls=%fused_computation | loop fusion | flops 4013184 | bytes 10752 | tf_op jit(solution)/shard_map/reduce_sum | solution.py:150
  36.9 1.8 %collective-permute-start.7 = (bf16[192,128]{1,0:T(8,128)(2,1)S(1)}, bf16[192,128]{1,0:T(8,128)(2,1)S(1)}, u32[]{:S(2)}, u32[]{:S(2)}) collective-permute-start(bf16[192,128]{1,0:T(8,128)(2,1)S(1)} %pad_maximum_fusion.3), channel_id=1, source_target_pairs={{0,2},{1,3},{2,0},{3,1},{4,6},{5,7},{6,4},{7,5},{8,14},{9,15},{10,... | collective-permute-start | bytes 147464 | tf_op jit(solution)/shard_map/ppermute | solution.py:36
  38.6 0.2 convolution_convert_fusion.3
  38.9 2.1 %collective-permute-done.7 = bf16[192,128]{1,0:T(8,128)(2,1)S(1)} collective-permute-done((bf16[192,128]{1,0:T(8,128)(2,1)S(1)}, bf16[192,128]{1,0:T(8,128)(2,1)S(1)}, u32[]{:S(2)}, u32[]{:S(2)}) %collective-permute-start.7) | collective-permute-done | bytes 49184 | tf_op jit(solution)/shard_map/ppermute | solution.py:36
  41.0 1.6 %collective-permute-start.9 = (bf16[320,128]{1,0:T(8,128)(2,1)S(1)}, bf16[320,128]{1,0:T(8,128)(2,1)S(1)}, u32[]{:S(2)}, u32[]{:S(2)}) collective-permute-start(bf16[320,128]{1,0:T(8,128)(2,1)S(1)} %pad_maximum_fusion.1), channel_id=1, source_target_pairs={{0,8},{8,0},{16,24},{24,16},{1,9},{9,1},{17,25},{25,17},{2,10},{10... | collective-permute-start | bytes 245768 | tf_op jit(solution)/shard_map/ppermute | solution.py:40
  42.6 1.2 %collective-permute-done.5 = bf16[448,128]{1,0:T(8,128)(2,1)S(1)} collective-permute-done((bf16[448,128]{1,0:T(8,128)(2,1)S(1)}, bf16[448,128]{1,0:T(8,128)(2,1)S(1)}, u32[]{:S(2)}, u32[]{:S(2)}) %collective-permute-start.5) | collective-permute-done | bytes 114720 | tf_op jit(solution)/shard_map/ppermute | solution.py:26
  43.8 0.0 collective-permute-done.6
  43.9 0.3 fusion.5
  44.3 0.1 convolution_convert_fusion
  44.4 0.5 fusion.9
  44.9 0.2 fusion.6
  45.1 0.0 copy-start.1
  45.1 0.1 collective-permute-start.10
  45.2 3.7 %collective-permute-done.10 = bf16[256,128]{1,0:T(8,128)(2,1)S(1)} collective-permute-done((bf16[256,128]{1,0:T(8,128)(2,1)S(1)}, bf16[256,128]{1,0:T(8,128)(2,1)S(1)}, u32[]{:S(2)}, u32[]{:S(2)}) %collective-permute-start.10) | collective-permute-done | bytes 65568 | tf_op jit(solution)/shard_map/ppermute | solution.py:193
  48.9 0.0 collective-permute-start.11
  48.9 3.7 %collective-permute-done.11 = bf16[256,128]{1,0:T(8,128)(2,1)S(1)} collective-permute-done((bf16[256,128]{1,0:T(8,128)(2,1)S(1)}, bf16[256,128]{1,0:T(8,128)(2,1)S(1)}, u32[]{:S(2)}, u32[]{:S(2)}) %collective-permute-start.11) | collective-permute-done | bytes 65568 | tf_op jit(solution)/shard_map/ppermute | solution.py:193
  52.6 0.0 collective-permute-start.12
  52.6 3.7 %collective-permute-done.12 = bf16[256,128]{1,0:T(8,128)(2,1)S(1)} collective-permute-done((bf16[256,128]{1,0:T(8,128)(2,1)S(1)}, bf16[256,128]{1,0:T(8,128)(2,1)S(1)}, u32[]{:S(2)}, u32[]{:S(2)}) %collective-permute-start.12) | collective-permute-done | bytes 65568 | tf_op jit(solution)/shard_map/ppermute | solution.py:193
  56.4 0.3 fusion.8
  56.7 0.7 %copy.14 = bf16[1,256,128]{2,1,0:T(8,128)(2,1)} copy(bf16[1,256,128]{1,2,0:T(8,128)(2,1)S(1)} %fusion.8) | data formatting | bytes 131072
  (70 shorter events, 0.7 us)
Async XLA Ops:
  0.6 14.7 %copy-start = (bf16[1,256,1024]{2,1,0:T(8,128)(2,1)S(1)}, bf16[1,256,1024]{2,1,0:T(8,128)(2,1)}, u32[]{:S(2)}) copy-start(bf16[1,256,1024]{2,1,0:T(8,128)(2,1)} %param.9) | copy-start | bytes 1572868
  0.6 14.7 %copy-start.5 = (bf16[1,256,128]{2,1,0:T(8,128)(2,1)S(1)}, bf16[1,256,128]{2,1,0:T(8,128)(2,1)}, u32[]{:S(2)}) copy-start(bf16[1,256,128]{2,1,0:T(8,128)(2,1)} %param.14) | copy-start | bytes 196612
  1.4 24.0 %collective-permute-start.4 = (bf16[16,128]{1,0:T(8,128)(2,1)S(1)}, bf16[16,128]{1,0:T(8,128)(2,1)S(1)}, u32[]{:S(2)}, u32[]{:S(2)}) collective-permute-start(bf16[16,128]{1,0:T(8,128)(2,1)S(1)} %pad.8), channel_id=1, source_target_pairs={{0,2},{1,3},{2,0},{3,1},{4,6},{5,7},{6,4},{7,5},{8,14},{9,15},{10,... | collective-permute-start | bytes 12296 | tf_op jit(solution)/shard_map/ppermute | solution.py:36
  5.4 18.8 %collective-permute-start.3 = (bf16[272,128]{1,0:T(8,128)(2,1)S(1)}, bf16[272,128]{1,0:T(8,128)(2,1)S(1)}, u32[]{:S(2)}, u32[]{:S(2)}) collective-permute-start(bf16[272,128]{1,0:T(8,128)(2,1)S(1)} %pad_maximum_fusion.2), channel_id=1, source_target_pairs={{0,7},{1,2},{2,1},{3,4},{4,3},{5,6},{6,5},{7,0},{8,15},{9,10},{10,... | collective-permute-start | bytes 208904 | tf_op jit(solution)/shard_map/ppermute | solution.py:26
  8.8 15.4 %collective-permute-start.2 = (bf16[272,128]{1,0:T(8,128)(2,1)S(1)}, bf16[272,128]{1,0:T(8,128)(2,1)S(1)}, u32[]{:S(2)}, u32[]{:S(2)}) collective-permute-start(bf16[272,128]{1,0:T(8,128)(2,1)S(1)} %pad_maximum_fusion.2), channel_id=1, source_target_pairs={{0,1},{1,0},{2,3},{3,2},{4,5},{5,4},{6,7},{7,6},{8,9},{9,8},{10,11... | collective-permute-start | bytes 208904 | tf_op jit(solution)/shard_map/ppermute | solution.py:26
  15.3 3.5 %copy-start.7 = (s32[1,4]{1,0:T(1,128)S(1)}, s32[1,4]{1,0:T(1,128)}, u32[]{:S(2)}) copy-start(s32[1,4]{1,0:T(1,128)} %param.15) | copy-start | bytes 52
  15.4 8.4 %copy-start.6 = (s32[1,256]{1,0:T(1,128)S(1)}, s32[1,256]{1,0:T(1,128)}, u32[]{:S(2)}) copy-start(s32[1,256]{1,0:T(1,128)} %param.16) | copy-start | bytes 3076
  15.4 8.6 %copy-start.4 = (bf16[1,256,128]{2,1,0:T(8,128)(2,1)S(1)}, bf16[1,256,128]{2,1,0:T(8,128)(2,1)}, u32[]{:S(2)}) copy-start(bf16[1,256,128]{2,1,0:T(8,128)(2,1)} %param.11) | copy-start | bytes 196612
  15.7 7.2 %collective-permute-start.1 = (bf16[256,128]{1,0:T(8,128)(2,1)S(1)}, bf16[256,128]{1,0:T(8,128)(2,1)S(1)}, u32[]{:S(2)}, u32[]{:S(2)}) collective-permute-start(bf16[256,128]{1,0:T(8,128)(2,1)S(1)} %get-tuple-element.63), channel_id=1, source_target_pairs={{0,7},{1,2},{2,1},{3,4},{4,3},{5,6},{6,5},{7,0},{8,15},{9,10},{10,... | collective-permute-start | bytes 196616 | tf_op jit(solution)/shard_map/ppermute | solution.py:26
  18.2 5.5 %collective-permute-start = (bf16[256,128]{1,0:T(8,128)(2,1)S(1)}, bf16[256,128]{1,0:T(8,128)(2,1)S(1)}, u32[]{:S(2)}, u32[]{:S(2)}) collective-permute-start(bf16[256,128]{1,0:T(8,128)(2,1)S(1)} %get-tuple-element.63), channel_id=1, source_target_pairs={{0,1},{1,0},{2,3},{3,2},{4,5},{5,4},{6,7},{7,6},{8,9},{9,8},{10,11... | collective-permute-start | bytes 196616 | tf_op jit(solution)/shard_map/ppermute | solution.py:26
  20.1 4.9 %copy-start.3 = (bf16[1,192,768]{2,1,0:T(8,128)(2,1)S(1)}, bf16[1,192,768]{2,1,0:T(8,128)(2,1)}, u32[]{:S(2)}) copy-start(bf16[1,192,768]{2,1,0:T(8,128)(2,1)} %param.12) | copy-start | bytes 884740
  31.9 1.1 %copy-start.2 = (bf16[1,256,1024]{2,1,0:T(8,128)(2,1)S(1)}, bf16[1,256,1024]{2,1,0:T(8,128)(2,1)}, u32[]{:S(2)}) copy-start(bf16[1,256,1024]{2,1,0:T(8,128)(2,1)} %param.10) | copy-start | bytes 1572868
  32.0 7.0 %collective-permute-start.8 = (bf16[128,128]{1,0:T(8,128)(2,1)S(1)}, bf16[128,128]{1,0:T(8,128)(2,1)S(1)}, u32[]{:S(2)}, u32[]{:S(2)}) collective-permute-start(bf16[128,128]{1,0:T(8,128)(2,1)S(1)} %slice_reduce_fusion), channel_id=1, source_target_pairs={{0,3},{1,6},{2,5},{3,0},{4,7},{5,2},{6,1},{7,4},{8,13},{9,12},{10,... | collective-permute-start | bytes 98312 | tf_op jit(solution)/shard_map/ppermute | solution.py:36
  33.3 10.5 %collective-permute-start.6 = (bf16[448,128]{1,0:T(8,128)(2,1)S(1)}, bf16[448,128]{1,0:T(8,128)(2,1)S(1)}, u32[]{:S(2)}, u32[]{:S(2)}) collective-permute-start(bf16[448,128]{1,0:T(8,128)(2,1)S(1)} %pad_maximum_fusion), channel_id=1, source_target_pairs={{0,7},{1,2},{2,1},{3,4},{4,3},{5,6},{6,5},{7,0},{8,15},{9,10},{10,... | collective-permute-start | bytes 344072 | tf_op jit(solution)/shard_map/ppermute | solution.py:26
  36.0 7.8 %collective-permute-start.5 = (bf16[448,128]{1,0:T(8,128)(2,1)S(1)}, bf16[448,128]{1,0:T(8,128)(2,1)S(1)}, u32[]{:S(2)}, u32[]{:S(2)}) collective-permute-start(bf16[448,128]{1,0:T(8,128)(2,1)S(1)} %pad_maximum_fusion), channel_id=1, source_target_pairs={{0,1},{1,0},{2,3},{3,2},{4,5},{5,4},{6,7},{7,6},{8,9},{9,8},{10,11... | collective-permute-start | bytes 344072 | tf_op jit(solution)/shard_map/ppermute | solution.py:26
  36.9 4.2 %collective-permute-start.7 = (bf16[192,128]{1,0:T(8,128)(2,1)S(1)}, bf16[192,128]{1,0:T(8,128)(2,1)S(1)}, u32[]{:S(2)}, u32[]{:S(2)}) collective-permute-start(bf16[192,128]{1,0:T(8,128)(2,1)S(1)} %pad_maximum_fusion.3), channel_id=1, source_target_pairs={{0,2},{1,3},{2,0},{3,1},{4,6},{5,7},{6,4},{7,5},{8,14},{9,15},{10,... | collective-permute-start | bytes 147464 | tf_op jit(solution)/shard_map/ppermute | solution.py:36
  41.0 2.8 %collective-permute-start.9 = (bf16[320,128]{1,0:T(8,128)(2,1)S(1)}, bf16[320,128]{1,0:T(8,128)(2,1)S(1)}, u32[]{:S(2)}, u32[]{:S(2)}) collective-permute-start(bf16[320,128]{1,0:T(8,128)(2,1)S(1)} %pad_maximum_fusion.1), channel_id=1, source_target_pairs={{0,8},{8,0},{16,24},{24,16},{1,9},{9,1},{17,25},{25,17},{2,10},{10... | collective-permute-start | bytes 245768 | tf_op jit(solution)/shard_map/ppermute | solution.py:40
  45.1 11.3 %copy-start.1 = (bf16[256,128]{1,0:T(8,128)(2,1)}, bf16[256,128]{1,0:T(8,128)(2,1)S(1)}, u32[]{:S(2)}) copy-start(bf16[256,128]{1,0:T(8,128)(2,1)S(1)} %fusion.6) | copy-start | bytes 196612
  45.1 3.7 %collective-permute-start.10 = (bf16[256,128]{1,0:T(8,128)(2,1)S(1)}, bf16[256,128]{1,0:T(8,128)(2,1)S(1)}, u32[]{:S(2)}, u32[]{:S(2)}) collective-permute-start(bf16[256,128]{1,0:T(8,128)(2,1)S(1)} %fusion.6), channel_id=1, source_target_pairs={{0,8},{8,16},{16,24},{24,0},{1,9},{9,17},{17,25},{25,1},{2,10},{10... | collective-permute-start | bytes 196616 | tf_op jit(solution)/shard_map/ppermute | solution.py:193
  48.9 3.7 %collective-permute-start.11 = (bf16[256,128]{1,0:T(8,128)(2,1)S(1)}, bf16[256,128]{1,0:T(8,128)(2,1)S(1)}, u32[]{:S(2)}, u32[]{:S(2)}) collective-permute-start(bf16[256,128]{1,0:T(8,128)(2,1)S(1)} %collective-permute-done.10), channel_id=1, source_target_pairs={{0,8},{8,16},{16,24},{24,0},{1,9},{9,17},{17,25},{25,1},{2,10},{10... | collective-permute-start | bytes 196616 | tf_op jit(solution)/shard_map/ppermute | solution.py:193
  52.6 3.7 %collective-permute-start.12 = (bf16[256,128]{1,0:T(8,128)(2,1)S(1)}, bf16[256,128]{1,0:T(8,128)(2,1)S(1)}, u32[]{:S(2)}, u32[]{:S(2)}) collective-permute-start(bf16[256,128]{1,0:T(8,128)(2,1)S(1)} %collective-permute-done.11), channel_id=1, source_target_pairs={{0,8},{8,16},{16,24},{24,0},{1,9},{9,17},{17,25},{25,1},{2,10},{10... | collective-permute-start | bytes 196616 | tf_op jit(solution)/shard_map/ppermute | solution.py:193
